TPU v7x, 512 devices: a whole 4x4x16 slice. The times are simulated.
512 devices in a mesh: field: 32 (over z_hi, x, core), point: 16 (over y, z_lo).
Axes of the slice: x: 4, y: 4, z: 16 (z_hi: 4, z_lo: 4; z = z_hi * 4 + z_lo), core: 2. Of those that a mesh axis runs over, the one named last changes fastest.
Arguments:
- residual_in: bfloat16 [32, 4096, 2048], P('field', 'point'), may hold values from -6 to 6
- coefs_in: bfloat16 [32, 4096, 4, 256], P('field', 'point'), may hold values from 0 to 1
- dictionary: bfloat16 [8192, 2048], P('field'), may hold values from -0.125 to 0.125
- owner_order: int32 [32], replicated, may hold values from 0 to 31, each once
- pixel_of: int32 [32, 4096], P('field', 'point'), may hold values from 0 to 4095, each once within a row
Outputs:
- maps: float32 [32, 4, 256, 32, 128], P('field', None, 'point')
Inputs may be any that keep to these rules, and one draw needn't show every extreme that they name: `owner_order`: A permutation of the dictionary blocks. `pixel_of`: each field's row is a permutation of its scan points over the 32 x 128 pixels.
All inputs are finite; a program needn't handle non-finite values.
Results may differ from a plain program's by a relative error of at most 0.00045.
Values may be sent and summed in bfloat16 or wider, within the bound.
A program may use at most 64 MiB of HBM per device.

v0:
```python
import jax
import jax.numpy as jnp
from jax import lax
from jax.sharding import PartitionSpec as P

TURNS = 4
SWEEPS = 4
MAP_W = 128
time_step = 0.2
edge_scale = 0.5


def from_root(value, axis, source):
    kept = jnp.where(lax.axis_index(axis) == source, value, 0).astype(value.dtype)
    return lax.psum(kept, axis)


def block_steps(templates):
    gram = lax.dot_general(
        templates, templates, (((1,), (1,)), ((), ())), preferred_element_type=jnp.float32
    )
    return 1.0 / jnp.sum(jnp.abs(gram), axis=1)


def diffuse(grids):
    for repeat in range(SWEEPS):
        padded = jnp.pad(grids, ((0, 0), (1, 1), (1, 1)), mode="edge")
        summed = jnp.zeros_like(grids)
        for neighbour in (
            padded[:, :-2, 1:-1],
            padded[:, 2:, 1:-1],
            padded[:, 1:-1, :-2],
            padded[:, 1:-1, 2:],
        ):
            differ = neighbour - grids
            scaled = differ / edge_scale
            summed = summed + differ / (1.0 + scaled * scaled)
        grids = grids + time_step * summed
    return grids


def build_maps(moved, pixel_ids):
    points = moved.shape[0]
    count = moved.shape[1]
    local_kb = moved.shape[2]
    values = moved.reshape(points, count * local_kb).T
    flat = jnp.zeros((count * local_kb, points), jnp.float32).at[:, pixel_ids].set(values)
    grids = diffuse(flat.reshape(count * local_kb, points // MAP_W, MAP_W))
    return grids.reshape(count, local_kb, points // MAP_W, MAP_W)


def per_device(residual_in, coefs_in, dictionary, owner_order, pixel_of):
    residual = residual_in[0]
    coefs = coefs_in[0].astype(jnp.float32)
    pixel_ids = lax.all_gather(pixel_of[0], "point", axis=0, tiled=True)
    updated = []
    for turn_index in range(TURNS):
        owner = owner_order[turn_index]
        templates = from_root(dictionary, "field", owner)
        step_size = block_steps(templates)
        correlation = lax.dot_general(
            residual, templates, (((1,), (1,)), ((), ())), preferred_element_type=jnp.float32
        )
        before = coefs[:, turn_index, :]
        after = jnp.maximum(before + step_size[None, :] * correlation, 0.0)
        updated.append(after)
        if turn_index + 1 < TURNS:
            change = (after - before).astype(jnp.bfloat16)
            residual = (
                residual.astype(jnp.float32)
                - jnp.dot(change, templates, preferred_element_type=jnp.float32)
            ).astype(jnp.bfloat16)
    stacked = jnp.stack(updated, axis=1)
    maps = build_maps(
        lax.all_to_all(stacked, "point", split_axis=2, concat_axis=0, tiled=True), pixel_ids
    )
    return maps[None]


def solution(mesh):
    placed = (
        P("field", "point", None),
        P("field", "point", None, None),
        P("field", None),
        P(),
        P("field", "point"),
    )
    return jax.shard_map(
        per_device,
        mesh=mesh,
        in_specs=placed,
        out_specs=P("field", None, "point", None, None),
        check_vma=False,
    )
```

profile of v0, /device:TPU:32, one launch (start us, length us, event | category | flops | bytes accessed | tf_op | source)
XLA Modules:
  0.0 503.0 jit_solution(4180003535699886071)
XLA Ops:
  6.5 1.5 fusion.46
  10.5 3.3 broadcast_select_fusion.3
  13.9 1.0 copy-done.4
  15.3 382.6 %all-reduce.3.cloned.1.call-done = (bf16[256,2048]{1,0:T(8,128)(2,1)}, bf16[256,2048]{1,0:T(8,128)(2,1)}, bf16[256,2048]{1,0:T(8,128)(2,1)}, bf16[256,2048]{1,0:T(8,128)(2,1)}) async-done(((bf16[256,2048]{1,0:T(8,128)(2,1)}, bf16[256,2048]{1,0:T(8,128)(2,1)}, bf16[256,2048]{1,0:T(8,128)(2,1)}, bf16[256,2048]{1,0:T(8,128)(2,1)}), (bf16[256,2048]{1,0:T(8,128)(2,1)}, bf16[256,2048]{1,0:T(8,128)(2,1)}, ...) | async-done | bytes 4194320 | tf_op jit(solution)/shard_map/psum | solution.py:15
  397.9 2.1 fusion.15
  400.1 0.5 fusion.14
  401.1 0.7 copy-done.1
  401.8 0.5 fusion.16
  403.3 0.7 copy-done.3
  404.0 0.5 fusion.17
  404.6 0.5 fusion.18
  405.5 2.5 fusion.7
  408.1 1.6 copy.31
  409.8 9.9 %all-to-all-start = ((f32[256,4,256]{0,1,2:T(4,128)}), f32[256,4,256]{0,1,2:T(4,128)S(1)}, u32[]{:S(2)}, u32[]{:S(2)}) async-start(f32[256,4,256]{0,1,2:T(4,128)} %copy.31), calls=%async_computation | async-start | bytes 2097152 | tf_op jit(solution)/shard_map/all_to_all | solution.py:75
  419.6 49.2 %all-gather = s32[1,4096]{1,0:T(1,128)S(1)} all-gather(s32[1,256]{1,0:T(1,128)S(1)} %copy-done.5), channel_id=2, replica_groups=mesh['field'=32,'point'=16] {'point'}, dimensions={1}, use_global_device_ids=true | all-gather | bytes 17408 | tf_op jit(solution)/shard_map/all_gather | solution.py:55
  468.9 0.6 copy.32
  469.5 0.6 copy.39
  470.1 2.0 copy.33
  472.1 11.6 %scatter_custom_fusion = f32[64,4096]{0,1:T(8,128)S(1)} fusion(s32[4096]{0:T(1024)S(1)} %compare_select_fusion, f32[4096,64]{1,0:T(8,128)} %copy.33, f32[]{:T(128)} %constant.31.clone.1), kind=kCustom, calls=%fused_computation.88 | custom fusion | bytes 1049088 | tf_op jit(solution)/shard_map/scatter | solution.py:47
  483.7 0.9 copy.38
  485.3 2.0 multiply_add_fusion.3
  488.0 2.0 multiply_add_fusion.2
  490.7 2.0 multiply_add_fusion.1
  493.4 2.8 multiply_add_fusion
  (38 shorter events, 5.1 us)
Async XLA Ops:
  6.5 391.4 %all-reduce.3.cloned.1.call-start = ((), (), s32[]{:S(2)}) async-start(), calls=%async_computation.1 | async-start | bytes 8388608 | tf_op jit(solution)/shard_map/psum | solution.py:15
  13.8 1.0 copy-start.4
  15.3 384.8 %copy-start = (bf16[1,256,2048]{2,1,0:T(8,128)(2,1)S(1)}, bf16[1,256,2048]{2,1,0:T(8,128)(2,1)}, u32[]{:S(2)}) copy-start(bf16[1,256,2048]{2,1,0:T(8,128)(2,1)} %param.5) | copy-start | bytes 3145732
  397.9 2.1 copy-start.2
  400.6 1.2 copy-start.1
  402.8 1.2 copy-start.3
  403.3 1.3 copy-start.6
  409.8 9.9 %copy-start.5 = (s32[1,256]{1,0:T(1,128)S(1)}, s32[1,256]{1,0:T(1,128)}, u32[]{:S(2)}) copy-start(s32[1,256]{1,0:T(1,128)} %param.9) | copy-start | bytes 3076
  409.8 59.1 %all-to-all-start = ((f32[256,4,256]{0,1,2:T(4,128)}), f32[256,4,256]{0,1,2:T(4,128)S(1)}, u32[]{:S(2)}, u32[]{:S(2)}) async-start(f32[256,4,256]{0,1,2:T(4,128)} %copy.31), calls=%async_computation | async-start | bytes 2097152 | tf_op jit(solution)/shard_map/all_to_all | solution.py:75
Sparse Core Ops, SparseCore 0:
  14.0 383.9 all-reduce.2
where the time goes:
time: 503 us
  waiting for transfers between devices  383 us (76%)
  blocking collectives  49.2 us (10%)
  local copies, waits for them, and re-layouts  23.6 us (5%)
  between operations  16.2 us (3%)
  other arithmetic  13.1 us (3%)
  starting transfers between devices  9.86 us (2%)
  matrix products  8.38 us (2%)
    psum x1, waiting for transfers between devices, from_root(): return lax.psum(kept, axis)  383 us
    all_gather x1, blocking collectives, per_device(): pixel_ids = lax.all_gather(pixel_of[0], 'point', axis=0, tiled=True)  49.2 us
    scatter x1, local copies, waits for them, and re-layouts, build_maps(): jnp.zeros((count * local_kb, points), jnp.float32).at[:, pixel_ids]  11.6 us
  transfers between devices with their start and end apart: 2, of which 1 were waited for; matrix products, arithmetic and copies ran while one was open for 0% of the time, Pallas kernels for 0%

commit v1 on v0

--- a/solution.py
+++ b/solution.py
@@ -52,7 +52,9 @@
 def per_device(residual_in, coefs_in, dictionary, owner_order, pixel_of):
     residual = residual_in[0]
     coefs = coefs_in[0].astype(jnp.float32)
-    pixel_ids = lax.all_gather(pixel_of[0], "point", axis=0, tiled=True)
+    pixel_ids = jnp.concatenate(
+        lax.all_to_all(jnp.stack([pixel_of[0]] * lax.axis_size("point")), "point", 0, 0), axis=0
+    )
     updated = []
     for turn_index in range(TURNS):
         owner = owner_order[turn_index]

time: 503 us -> 477 us (0.948)
  the two profiles are of different devices: /device:TPU:32 before, /device:TPU:1 now
where the time goes in v1:
time: 477 us
  waiting for transfers between devices  398 us (83%)
  local copies, waits for them, and re-layouts  23.8 us (5%)
  starting transfers between devices  17.8 us (4%)
  between operations  16.2 us (3%)
  other arithmetic  13.1 us (3%)
  matrix products  8.39 us (2%)
    psum x1, waiting for transfers between devices, from_root(): return lax.psum(kept, axis)  371 us
    all_to_all x1, waiting for transfers between devices, per_device(): lax.all_to_all(stacked, 'point', split_axis=2, concat_axis=0, tiled=True)  26.2 us
    scatter x1, local copies, waits for them, and re-layouts, build_maps(): jnp.zeros((count * local_kb, points), jnp.float32).at[:, pixel_ids]  11.6 us
  transfers between devices with their start and end apart: 3, of which 2 were waited for; matrix products, arithmetic and copies ran while one was open for 2% of the time, Pallas kernels for 0%

profile of v1, /device:TPU:1, one launch (start us, length us, event | category | flops | bytes accessed | tf_op | source)
XLA Modules:
  0.0 477.0 jit_solution(15779494919038092413)
XLA Ops:
  6.5 1.5 fusion.46
  10.5 3.3 broadcast_select_fusion.3
  13.9 0.7 copy-done.5
  14.5 0.6 stack.18
  15.1 9.2 %all-to-all-start = ((s32[16,1,256]{2,1,0:T(1,128)}), s32[16,1,256]{2,1,0:T(1,128)S(1)}, u32[]{:S(2)}, u32[]{:S(2)}) async-start(s32[16,1,256]{2,1,0:T(1,128)} %stack.18), calls=%async_computation | async-start | bytes 32768 | tf_op jit(solution)/shard_map/all_to_all | solution.py:56
  24.8 371.5 %all-reduce.3.cloned.1.call-done = (bf16[256,2048]{1,0:T(8,128)(2,1)}, bf16[256,2048]{1,0:T(8,128)(2,1)}, bf16[256,2048]{1,0:T(8,128)(2,1)}, bf16[256,2048]{1,0:T(8,128)(2,1)}) async-done(((bf16[256,2048]{1,0:T(8,128)(2,1)}, bf16[256,2048]{1,0:T(8,128)(2,1)}, bf16[256,2048]{1,0:T(8,128)(2,1)}, bf16[256,2048]{1,0:T(8,128)(2,1)}), (bf16[256,2048]{1,0:T(8,128)(2,1)}, bf16[256,2048]{1,0:T(8,128)(2,1)}, ...) | async-done | bytes 4194320 | tf_op jit(solution)/shard_map/psum | solution.py:15
  396.3 2.1 fusion.15
  399.4 0.7 copy-done.1
  400.1 0.5 fusion.16
  401.6 0.7 copy-done.3
  402.9 0.5 fusion.18
  403.9 2.5 fusion.7
  406.4 1.6 copy.31
  408.1 8.6 %all-to-all-start.1 = ((f32[256,4,256]{0,1,2:T(4,128)}), f32[256,4,256]{0,1,2:T(4,128)S(1)}, u32[]{:S(2)}, u32[]{:S(2)}) async-start(f32[256,4,256]{0,1,2:T(4,128)} %copy.31), calls=%async_computation.1 | async-start | bytes 2097152 | tf_op jit(solution)/shard_map/all_to_all | solution.py:77
  416.7 26.2 %all-to-all-done.1 = f32[256,4,256]{0,1,2:T(4,128)S(1)} async-done(((f32[256,4,256]{0,1,2:T(4,128)}), f32[256,4,256]{0,1,2:T(4,128)S(1)}, u32[]{:S(2)}, u32[]{:S(2)}) %all-to-all-start.1) | async-done | bytes 1048608 | tf_op jit(solution)/shard_map/all_to_all | solution.py:77
  442.9 0.6 copy.32
  443.5 0.6 copy.39
  444.1 1.9 copy.33
  446.1 11.6 %scatter_custom_fusion = f32[64,4096]{0,1:T(8,128)S(1)} fusion(s32[4096]{0:T(1024)S(1)} %bitcast.85, f32[4096,64]{1,0:T(8,128)} %copy.33, f32[]{:T(128)} %constant.31.clone.1), kind=kCustom, calls=%fused_computation.88 | custom fusion | bytes 1049088 | tf_op jit(solution)/shard_map/scatter | solution.py:47
  457.7 0.9 copy.38
  459.3 2.0 multiply_add_fusion.3
  462.0 2.0 multiply_add_fusion.2
  464.7 2.0 multiply_add_fusion.1
  467.4 2.8 multiply_add_fusion
  (40 shorter events, 6.1 us)
Async XLA Ops:
  6.5 389.7 %all-reduce.3.cloned.1.call-start = ((), (), s32[]{:S(2)}) async-start(), calls=%async_computation.2 | async-start | bytes 8388608 | tf_op jit(solution)/shard_map/psum | solution.py:15
  13.8 0.7 copy-start.5
  13.8 10.5 %copy-start.4 = (bf16[1,256,4,256]{3,2,1,0:T(4,128)(2,1)S(1)}, bf16[1,256,4,256]{3,2,1,0:T(4,128)(2,1)}, u32[]{:S(2)}) copy-start(bf16[1,256,4,256]{3,2,1,0:T(4,128)(2,1)} %param.6) | copy-start | bytes 1572868
  15.1 393.0 %all-to-all-start = ((s32[16,1,256]{2,1,0:T(1,128)}), s32[16,1,256]{2,1,0:T(1,128)S(1)}, u32[]{:S(2)}, u32[]{:S(2)}) async-start(s32[16,1,256]{2,1,0:T(1,128)} %stack.18), calls=%async_computation | async-start | bytes 32768 | tf_op jit(solution)/shard_map/all_to_all | solution.py:56
  24.8 373.6 %copy-start = (bf16[1,256,2048]{2,1,0:T(8,128)(2,1)S(1)}, bf16[1,256,2048]{2,1,0:T(8,128)(2,1)}, u32[]{:S(2)}) copy-start(bf16[1,256,2048]{2,1,0:T(8,128)(2,1)} %param.5) | copy-start | bytes 3145732
  396.3 2.1 copy-start.2
  398.9 1.2 copy-start.1
  401.1 1.2 copy-start.3
  401.6 1.3 copy-start.6
  408.1 34.8 %all-to-all-start.1 = ((f32[256,4,256]{0,1,2:T(4,128)}), f32[256,4,256]{0,1,2:T(4,128)S(1)}, u32[]{:S(2)}, u32[]{:S(2)}) async-start(f32[256,4,256]{0,1,2:T(4,128)} %copy.31), calls=%async_computation.1 | async-start | bytes 2097152 | tf_op jit(solution)/shard_map/all_to_all | solution.py:77
Sparse Core Ops, SparseCore 0:
  14.0 382.2 all-reduce.2
